TPU v7x, 512 devices: a whole 4x4x16 slice. The times are simulated.
512 devices in a mesh: tile: 128 (over z, x, core), layer: 4 (over y).
Axes of the slice: x: 4, y: 4, z: 16, core: 2. Of those that a mesh axis runs over, the one named last changes fastest.
Arguments:
- head_start: float32 [8, 8192, 512], P('layer', 'tile'), may hold values from -2 to 0.5
- soil_class: int32 [8, 8192, 512], P('layer', 'tile'), may hold values from 0 to 11
- land_mask: int32 [8192, 512], P('tile'), may hold values 0 or 1
- ks_table: float32 [12], replicated, may hold values from 0.2 to 5
- alpha_table: float32 [12], replicated, may hold values from 0.5 to 2
- store_table: float32 [12], replicated, may hold values from 0.5 to 2
- section: float32 [2048, 128], P('tile'), may hold values from -6 to 6
- cross_owner: int32 [128, 256], P('tile'), may hold values from 0 to 127, as said below
- cross_local: int32 [128, 256], P('tile'), may hold values from 0 to 15
- node_cell: int32 [128, 256, 128], P('tile'), may hold values from -1 to 32767, as said below
- bed_cond: float32 [128, 256, 128], P('tile'), may hold values from 0.5 to 4
Outputs:
- head: float32 [8, 8192, 512], P('layer', 'tile')
- inflow: float32 [2048, 128], P('tile', 'layer')
Inputs may be any that keep to these rules, and one draw needn't show every extreme that they name: `cross_owner`: no strip's row names one owner in more than 2 slots, and in every row some owner is named in exactly 2 slots. `node_cell`: -1 marks a node outside the strip; other values index the strip's top-layer cells row-major over 64 x 512. In each strip the slots with nodes come first, the rest are padding with every node -1.
All inputs are finite; a program needn't handle non-finite values. No bound on the sum of `land_mask` on one device may be relied on, other than what follows from the above.
Results may differ from a plain program's by a relative error of at most 0.00002.
Values sent between devices are 32-bit elements; how exact they have to be, the bound alone decides.
A program may use at most 64 MiB of HBM per device.

v0:
```python
import jax
import jax.numpy as jnp
from jax import lax
from jax.sharding import PartitionSpec as P

ITERS = 2
SWEEPS = 3
LATERAL = 1.0
VERTICAL = 2.0
GRAVITY = 1.0
NEIGHBOURS = (
    (0, -1, VERTICAL),
    (0, 1, VERTICAL),
    (1, -1, LATERAL),
    (1, 1, LATERAL),
    (2, -1, LATERAL),
    (2, 1, LATERAL),
)


def with_halo(block, sides, width):
    for axis, dim in sides:
        count = lax.axis_size(axis)
        forward = [(i, i + 1) for i in range(count - 1)]
        backward = [(target, source) for source, target in forward]
        low = lax.ppermute(
            lax.slice_in_dim(block, block.shape[dim] - width, None, axis=dim), axis, forward
        )
        high = lax.ppermute(lax.slice_in_dim(block, 0, width, axis=dim), axis, backward)
        block = jnp.concatenate([low, block, high], axis=dim)
    return block


def from_root(value, axis, source):
    kept = jnp.where(lax.axis_index(axis) == source, value, 0).astype(value.dtype)
    return lax.psum(kept, axis)


def beside(padded, axis_id, step):
    spans = [slice(1, -1), slice(1, -1), slice(1, -1)]
    spans[axis_id] = slice(1 + step, padded.shape[axis_id] - 1 + step)
    return padded[tuple(spans)]


def neighbor_weights(cond_pad, open_pad):
    centre = cond_pad[1:-1, 1:-1, 1:-1]
    centre_open = open_pad[1:-1, 1:-1, 1:-1]
    result = []
    for axis_id, step, factor in NEIGHBOURS:
        far = beside(cond_pad, axis_id, step)
        far_open = beside(open_pad, axis_id, step)
        result.append(factor * 2.0 * centre_open * far_open / (centre + far))
    return result


def relax(head_pad, weights, store, head_old, riv_diag, riv_rhs):
    total = store * head_old
    diagonal_sum = store
    for weight, (axis_id, step, factor) in zip(weights, NEIGHBOURS):
        total = total + weight * beside(head_pad, axis_id, step)
        diagonal_sum = diagonal_sum + weight
    total = total + GRAVITY * (weights[0] - weights[1]) + riv_rhs
    return total / (diagonal_sum + riv_diag)


def lookup(values_table, classes):
    result = jnp.zeros(classes.shape, jnp.float32)
    for class_id in range(values_table.shape[0]):
        result = jnp.where(classes == class_id, values_table[class_id], result)
    return result


def pad_dims(field, chosen_dims):
    widths = [(1, 1) if place in chosen_dims else (0, 0) for place in range(field.ndim)]
    return jnp.pad(field, widths)


def pick_heads(top_head, cells):
    breadth = top_head.shape[1]
    slots, width = cells.shape
    group = 16
    grouped = cells.reshape(slots // group, group * width)
    columns = jnp.arange(breadth, dtype=jnp.int32)[None, :]

    def one_group(flat_cells):
        picked_rows = jnp.take(top_head, flat_cells // breadth, axis=0)
        hit = columns == (flat_cells % breadth)[:, None]
        return jnp.sum(jnp.where(hit, picked_rows, 0.0), axis=1)

    return lax.map(one_group, grouped).reshape(slots, width)


def on_device(
    head_start,
    soil_class,
    land_mask,
    ks_table,
    alpha_table,
    store_table,
    section,
    cross_owner,
    cross_local,
    node_cell,
    bed_cond,
):
    layers, across, breadth = head_start.shape
    reach_rows = section.shape[0]
    node_count = section.shape[1]
    tile_count = lax.axis_size("tile")
    quarter = node_count // lax.axis_size("layer")
    node_first = lax.axis_index("layer") * quarter
    ks = lookup(ks_table, soil_class)
    alpha = lookup(alpha_table, soil_class)
    store = lookup(store_table, soil_class)
    landf = land_mask.astype(jnp.float32)[None]
    owners = cross_owner[0]
    positions = cross_local[0]
    node_cells = node_cell[0]
    bed_given = bed_cond[0]
    whole_section = lax.all_gather(section, "tile", axis=0, tiled=True)
    slot_section = jnp.take(whole_section, owners * reach_rows + positions, axis=0)
    in_tile = node_cells >= 0
    flat_index = jnp.where(in_tile, node_cells, across * breadth)
    bed_terms = jnp.where(in_tile, bed_given, 0.0)
    diag_top = (
        jnp.zeros((across * breadth,), jnp.float32)
        .at[flat_index.reshape(-1)]
        .add(bed_terms.reshape(-1), mode="drop")
    )
    rhs_top = (
        jnp.zeros((across * breadth,), jnp.float32)
        .at[flat_index.reshape(-1)]
        .add((bed_terms * slot_section).reshape(-1), mode="drop")
    )
    top_diag = diag_top.reshape(across, breadth)
    top_rhs = rhs_top.reshape(across, breadth)
    head_old, ks_here, alpha_here, store_here, land_here = (head_start, ks, alpha, store, landf)
    on_top = (lax.axis_index("layer") == 0).astype(jnp.float32)
    riv_diag = jnp.zeros((layers, across, breadth), jnp.float32).at[0].set(top_diag * on_top)
    riv_rhs = jnp.zeros((layers, across, breadth), jnp.float32).at[0].set(top_rhs * on_top)

    def head_halo(field):
        return pad_dims(with_halo(field, (("tile", 1), ("layer", 0)), 1), (2,))

    head = head_old
    for picard in range(ITERS):
        head_pad = head_halo(head)
        conduct = ks_here * jnp.exp(alpha_here * jnp.minimum(head, 0.0))
        both_pad = pad_dims(
            with_halo(jnp.stack([conduct, conduct * land_here]), (("tile", 2), ("layer", 1)), 1),
            (3,),
        )
        cond_pad = both_pad[0]
        open_pad = both_pad[1]
        weights = neighbor_weights(cond_pad, open_pad)
        for sweep in range(SWEEPS):
            if sweep > 0:
                head_pad = head_halo(head)
            head = relax(head_pad, weights, store_here, head_old, riv_diag, riv_rhs)
    top_head = from_root(head[0], "layer", 0)
    my_cells = lax.dynamic_slice_in_dim(node_cells, node_first, quarter, 1)
    my_bed = lax.dynamic_slice_in_dim(bed_given, node_first, quarter, 1)
    my_section = lax.dynamic_slice_in_dim(slot_section, node_first, quarter, 1)
    my_inside = my_cells >= 0
    node_head = pick_heads(top_head, jnp.where(my_inside, my_cells, 0))
    slot_in = jnp.where(my_inside, my_bed * (node_head - my_section), 0.0)
    dense = (
        jnp.zeros((reach_rows * tile_count, quarter), jnp.float32)
        .at[owners * reach_rows + positions]
        .add(slot_in)
    )
    inflow = lax.psum_scatter(dense, "tile", scatter_dimension=0, tiled=True)
    return (head, inflow)


def solution(mesh):
    placed = (
        P("layer", "tile", None),
        P("layer", "tile", None),
        P("tile", None),
        P(),
        P(),
        P(),
        P("tile", None),
        P("tile", None),
        P("tile", None),
        P("tile", None, None),
        P("tile", None, None),
    )
    return jax.shard_map(
        on_device,
        mesh=mesh,
        in_specs=placed,
        out_specs=(P("layer", "tile", None), P("tile", "layer")),
        check_vma=False,
    )
```

profile of v0, /device:TPU:8, one launch (start us, length us, event | category | flops | bytes accessed | tf_op | source)
XLA Modules:
  0.0 1032.4 jit_solution(11896485293692213495)
XLA Ops:
  11.7 17.8 %fusion.107 = (f32[1,2,64,512]{3,2,1,0:T(8,128)S(1)}, f32[2,64,512]{2,1,0:T(8,128)S(1)}, f32[2,64,512]{2,1,0:T(8,128)S(1)}, pred[2,64,512]{2,1,0:T(8,128)(4,1)S(...) fusion(f32[2,64,512]{2,1,0:T(8,128)} %param.17, ...), kind=kLoop, calls=%fused_computation.316 | loop fusion | flops 2555904 | bytes 2097248 | tf_op jit(solution)/shard_map/stack | solution.py:150
  31.0 3.0 collective-permute-start
  35.3 3.6 collective-permute-start.4
  40.6 7.1 collective-permute-start.7
  49.8 3.9 collective-permute-start.3
  56.7 4.8 collective-permute-done.3
  61.5 3.4 collective-permute-done.2
  66.5 8.5 add_add_fusion.1
  76.1 104.6 %all-gather.2.cloned.1.call-done = f32[2048,128]{1,0:T(8,128)} async-done(((f32[16,128]{1,0:T(8,128)}), f32[2048,128]{1,0:T(8,128)}) %all-gather.2.cloned.1.call-update) | async-done | bytes 1048592 | tf_op jit(solution)/shard_map/all_gather | solution.py:120
  184.3 171.3 %scatter_custom_fusion.1 = f32[32768]{0:T(1024)S(1)} fusion(s32[32768]{0:T(1024)} %bitcast.101, f32[32768]{0:T(1024)S(1)} %get-tuple-element.136, f32[]{:T(128)} %constant.189.clone.1), kind=kCustom, calls=%fused_computation.302 | custom fusion | flops 32768 | bytes 131584 | tf_op jit(solution)/shard_map/scatter-add | solution.py:128
  357.3 171.2 %scatter_custom_fusion = f32[32768]{0:T(1024)S(1)} fusion(s32[32768]{0:T(1024)} %bitcast.102, f32[32768]{0:T(1024)} %get-tuple-element.134, f32[]{:T(128)} %constant.189.clone.1), kind=kCustom, calls=%fused_computation.304 | custom fusion | flops 32768 | bytes 131584 | tf_op jit(solution)/shard_map/scatter-add | solution.py:133
  540.3 3.4 collective-permute-start.10
  550.9 3.0 collective-permute-start.12
  556.7 3.9 collective-permute-start.14
  567.5 3.1 collective-permute-start.20
  572.0 5.1 collective-permute-start.16
  580.0 3.9 collective-permute-start.18
  585.9 4.1 collective-permute-start.22
  604.6 3.9 collective-permute-start.26
  613.7 4.8 collective-permute-start.28
  621.9 3.9 collective-permute-start.30
  630.5 75.9 %all-reduce.10.cloned.1.call-done = f32[64,512]{1,0:T(8,128)} async-done(((f32[64,512]{1,0:T(8,128)}), f32[64,512]{1,0:T(8,128)}) %all-reduce.10.cloned.1.call-update) | async-done | bytes 131088 | tf_op jit(solution)/shard_map/psum | solution.py:36
  706.4 54.5 %while.15 = (s32[]{:T(128)}, f32[16,512]{1,0:T(8,128)S(1)}, s32[16,512]{1,0:T(8,128)S(1)}, f32[64,512]{1,0:T(8,128)}, s32[]{:T(128)}, /*index=5*/s32[]{:T(128)}) while((s32[]{:T(128)}, f32[16,512]{1,0:T(8,128)S(1)}, s32[16,512]{1,0:T(8,128)S(1)}, f32[64,512]{1,0:T(8,128)}, s32[]{:T(128)}, /*index=5*/s32[]{:T(128)}) %tuple.130), condition=%wide.region_5.6_spmd.clone, body=%wide.region_3.5_spmd.clone.sunk | while | flops 1074690 | bytes 3175509 | solution.py:90
  763.6 262.3 %reduce-scatter.2.cloned.1.call-done = f32[16,32]{1,0:T(8,128)} async-done(((f32[2048,32]{1,0:T(8,128)}), f32[16,32]{1,0:T(8,128)}) %reduce-scatter.2.cloned.1.call-update) | async-done | bytes 2064 | tf_op jit(solution)/shard_map/reduce_scatter | solution.py:172
  (291 shorter events, 140.1 us)
Async XLA Ops:
  7.2 173.5 %all-gather.2.cloned.1.call-start = ((), (), s32[]{:S(2)}) async-start(), calls=%async_computation.1 | async-start | bytes 1056768 | tf_op jit(solution)/shard_map/all_gather | solution.py:120
  29.7 19.9 %collective-permute-start.1 = (f32[2,2,1,512]{3,2,1,0:T(1,128)S(1)}, f32[2,2,1,512]{3,2,1,0:T(1,128)S(1)}, u32[]{:S(2)}, u32[]{:S(2)}) collective-permute-start(f32[2,2,1,512]{3,2,1,0:T(1,128)S(1)} %get-tuple-element.168), channel_id=1, source_target_pairs={{4,0},{8,4},{12,8},{16,12},{20,16},{24,20},{28,24},{32,28},{36,32}... | collective-permute-start | bytes 24584 | tf_op jit(solution)/shard_map/ppermute | solution.py:29
  31.0 18.6 %collective-permute-start = (f32[2,2,1,512]{3,2,1,0:T(1,128)S(1)}, f32[2,2,1,512]{3,2,1,0:T(1,128)S(1)}, u32[]{:S(2)}, u32[]{:S(2)}) collective-permute-start(f32[2,2,1,512]{3,2,1,0:T(1,128)S(1)} %get-tuple-element.167), channel_id=1, source_target_pairs={{0,4},{4,8},{8,12},{12,16},{16,20},{20,24},{24,28},{28,32},{32,36}... | collective-permute-start | bytes 24584 | tf_op jit(solution)/shard_map/ppermute | solution.py:26
  39.0 667.3 %all-reduce.10.cloned.1.call-start = ((), (), s32[]{:S(2)}) async-start(), calls=%async_computation.2 | async-start | bytes 262144 | tf_op jit(solution)/shard_map/psum | solution.py:36
  40.6 15.8 %collective-permute-start.7 = (f32[1,66,512]{2,1,0:T(8,128)S(1)}, f32[1,66,512]{2,1,0:T(8,128)S(1)}, u32[]{:S(2)}, u32[]{:S(2)}) collective-permute-start(f32[1,66,512]{2,1,0:T(8,128)S(1)} %get-tuple-element.180), channel_id=1, source_target_pairs={{1,0},{2,1},{3,2},{5,4},{6,5},{7,6},{9,8},{10,9},{11,10},{13,12},{... | collective-permute-start | bytes 405512 | tf_op jit(solution)/shard_map/ppermute | solution.py:29
  47.7 8.7 collective-permute-start.6
  49.8 11.8 %collective-permute-start.3 = (f32[2,1,66,512]{3,2,1,0:T(8,128)S(1)}, f32[2,1,66,512]{3,2,1,0:T(8,128)S(1)}, u32[]{:S(2)}, u32[]{:S(2)}) collective-permute-start(f32[2,1,66,512]{3,2,1,0:T(8,128)S(1)} %get-tuple-element.164), channel_id=1, source_target_pairs={{1,0},{2,1},{3,2},{5,4},{6,5},{7,6},{9,8},{10,9},{11,10},{13,12},{... | collective-permute-start | bytes 811016 | tf_op jit(solution)/shard_map/ppermute | solution.py:29
  53.7 11.2 %collective-permute-start.2 = (f32[2,1,66,512]{3,2,1,0:T(8,128)S(1)}, f32[2,1,66,512]{3,2,1,0:T(8,128)S(1)}, u32[]{:S(2)}, u32[]{:S(2)}) collective-permute-start(f32[2,1,66,512]{3,2,1,0:T(8,128)S(1)} %get-tuple-element.163), channel_id=1, source_target_pairs={{0,1},{1,2},{2,3},{4,5},{5,6},{6,7},{8,9},{9,10},{10,11},{12,13},{... | collective-permute-start | bytes 811016 | tf_op jit(solution)/shard_map/ppermute | solution.py:26
  537.9 8.2 collective-permute-start.11
  540.3 8.4 collective-permute-start.10
  554.8 7.9 collective-permute-start.15
  556.7 7.9 collective-permute-start.14
  566.2 10.9 %collective-permute-start.21 = (f32[2,1,512]{2,1,0:T(1,128)S(1)}, f32[2,1,512]{2,1,0:T(1,128)S(1)}, u32[]{:S(2)}, u32[]{:S(2)}) collective-permute-start(f32[2,1,512]{2,1,0:T(1,128)S(1)} %get-tuple-element.186), channel_id=1, source_target_pairs={{4,0},{8,4},{12,8},{16,12},{20,16},{24,20},{28,24},{32,28},{36,32}... | collective-permute-start | bytes 12296 | tf_op jit(solution)/shard_map/ppermute | solution.py:29
  567.5 9.6 collective-permute-start.20
  570.7 6.5 collective-permute-start.17
  578.0 16.8 %collective-permute-start.19 = (f32[2,1,66,512]{3,2,1,0:T(8,128)S(1)}, f32[2,1,66,512]{3,2,1,0:T(8,128)S(1)}, u32[]{:S(2)}, u32[]{:S(2)}) collective-permute-start(f32[2,1,66,512]{3,2,1,0:T(8,128)S(1)} %get-tuple-element.162), channel_id=1, source_target_pairs={{1,0},{2,1},{3,2},{5,4},{6,5},{7,6},{9,8},{10,9},{11,10},{13,12},{... | collective-permute-start | bytes 811016 | tf_op jit(solution)/shard_map/ppermute | solution.py:29
  580.0 14.9 %collective-permute-start.18 = (f32[2,1,66,512]{3,2,1,0:T(8,128)S(1)}, f32[2,1,66,512]{3,2,1,0:T(8,128)S(1)}, u32[]{:S(2)}, u32[]{:S(2)}) collective-permute-start(f32[2,1,66,512]{3,2,1,0:T(8,128)S(1)} %get-tuple-element.161), channel_id=1, source_target_pairs={{0,1},{1,2},{2,3},{4,5},{5,6},{6,7},{8,9},{9,10},{10,11},{12,13},{... | collective-permute-start | bytes 811016 | tf_op jit(solution)/shard_map/ppermute | solution.py:26
  583.9 8.7 collective-permute-start.23
  585.9 8.7 collective-permute-start.22
  602.6 7.0 collective-permute-start.27
  604.6 7.0 collective-permute-start.26
  620.0 7.2 collective-permute-start.31
  621.9 7.0 collective-permute-start.30
  630.4 395.5 %reduce-scatter.2.cloned.1.call-start = ((), (), s32[]{:S(2)}) async-start(), calls=%async_computation.3 | async-start | bytes 1056768 | tf_op jit(solution)/shard_map/reduce_scatter | solution.py:172
  (35 other events, 568.2 us)
Sparse Core Ops, SparseCore 0:
  39.1 141.4 all-gather.1
  630.6 75.7 all-reduce.9
  763.7 262.1 reduce-scatter.1
where the time goes:
time: 1030 us
  waiting for transfers between devices  475 us (46%)
  other arithmetic  393 us (38%)
  starting transfers between devices  89.4 us (9%)
  local copies, waits for them, and re-layouts  59.6 us (6%)
  between operations  14.7 us (1%)
    reduce_scatter x1, waiting for transfers between devices, on_device(): inflow = lax.psum_scatter(dense, 'tile', scatter_dimension=0, tiled=True)  262 us
    scatter-add x1, other arithmetic, on_device(): diag_top = jnp.zeros((across * breadth,), jnp.float32).at[flat_index.resh...  171 us
    scatter-add x1, other arithmetic, on_device(): rhs_top = jnp.zeros((across * breadth,), jnp.float32).at[flat_index.resha...  171 us
    all_gather x1, waiting for transfers between devices, on_device(): whole_section = lax.all_gather(section, 'tile', axis=0, tiled=True)  105 us
    psum x1, waiting for transfers between devices, from_root(): return lax.psum(kept, axis)  75.9 us
    ppermute x16, starting transfers between devices, with_halo(): lax.ppermute(lax.slice_in_dim(block, block.shape[dim] - width, None, axis...  55.8 us
    gather x16, local copies, waits for them, and re-layouts, one_group(): picked_rows = jnp.take(top_head, flat_cells // breadth, axis=0)  47 us
    ppermute x16, starting transfers between devices, with_halo(): lax.ppermute(lax.slice_in_dim(block, 0, width, axis=dim), axis, backward)  33.4 us
  transfers between devices with their start and end apart: 35, of which 20 were waited for; matrix products, arithmetic and copies ran while one was open for 1% of the time, Pallas kernels for 0%

commit v1 on v0

--- a/solution.py
+++ b/solution.py
@@ -33,7 +33,10 @@
 
 def from_root(value, axis, source):
     kept = jnp.where(lax.axis_index(axis) == source, value, 0).astype(value.dtype)
-    return lax.psum(kept, axis)
+    _produce_sections = lambda unit, named_axis: jnp.sum(
+        jax.lax.all_gather(unit, named_axis), axis=0
+    )
+    return _produce_sections(kept, axis)
 
 
 def beside(padded, axis_id, step):

time: 1030 us -> 969 us (0.941)
  waiting for transfers between devices: 475 us -> 417 us
  local copies, waits for them, and re-layouts: 59.6 us -> 38.6 us
  blocking collectives: 0 us -> 13.9 us
    psum x1 -> x0, waiting for transfers between devices: 75.9 us -> none  [from_root(): return lax.psum(kept, axis)]
    gather x16, local copies, waits for them, and re-layouts: 47 us -> 25.9 us  [one_group(): picked_rows = jnp.take(top_head, flat_cells // breadth, axis=0)]
    reduce_scatter x1, waiting for transfers between devices: 262 us -> 281 us  [on_device(): inflow = lax.psum_scatter(dense, 'tile', scatter_dimension=0, tiled=True)]
    all_gather x0 -> x1, blocking collectives: none -> 13.9 us  [from_root(): jax.lax.all_gather(unit, named_axis)]
  transfers between devices with their start and end apart: 35 -> 34, of which waited for: 20 -> 19; matrix products, arithmetic and copies ran while one was open for 1% -> 1% of each run, Pallas kernels for 0% -> 0%
where the time goes in v1:
time: 969 us; the launch traced here: 967 us
  waiting for transfers between devices  417 us (43%)
  other arithmetic  392 us (40%)
  starting transfers between devices  89.3 us (9%)
  local copies, waits for them, and re-layouts  38.6 us (4%)
  between operations  15.1 us (2%)
  blocking collectives  13.9 us (1%)
    reduce_scatter x1, waiting for transfers between devices, on_device(): inflow = lax.psum_scatter(dense, 'tile', scatter_dimension=0, tiled=True)  281 us
    scatter-add x1, other arithmetic, on_device(): diag_top = jnp.zeros((across * breadth,), jnp.float32).at[flat_index.resh...  171 us
    scatter-add x1, other arithmetic, on_device(): rhs_top = jnp.zeros((across * breadth,), jnp.float32).at[flat_index.resha...  171 us
    all_gather x1, waiting for transfers between devices, on_device(): whole_section = lax.all_gather(section, 'tile', axis=0, tiled=True)  105 us
    ppermute x16, starting transfers between devices, with_halo(): lax.ppermute(lax.slice_in_dim(block, block.shape[dim] - width, None, axis...  55.8 us
    ppermute x16, starting transfers between devices, with_halo(): lax.ppermute(lax.slice_in_dim(block, 0, width, axis=dim), axis, backward)  33.4 us
    gather x16, local copies, waits for them, and re-layouts, one_group(): picked_rows = jnp.take(top_head, flat_cells // breadth, axis=0)  25.9 us
  transfers between devices with their start and end apart: 34, of which 19 were waited for; matrix products, arithmetic and copies ran while one was open for 1% of the time, Pallas kernels for 0%

profile of v1, /device:TPU:8, one launch (start us, length us, event | category | flops | bytes accessed | tf_op | source)
XLA Modules:
  0.0 967.5 jit_solution(8029153332786504947)
XLA Ops:
  11.8 17.8 %fusion.106 = (f32[1,2,64,512]{3,2,1,0:T(8,128)S(1)}, f32[2,64,512]{2,1,0:T(8,128)S(1)}, f32[2,64,512]{2,1,0:T(8,128)S(1)}, pred[2,64,512]{2,1,0:T(8,128)(4,1)S(...) fusion(f32[2,64,512]{2,1,0:T(8,128)} %param.17, ...), kind=kLoop, calls=%fused_computation.315 | loop fusion | flops 2555904 | bytes 2097248 | tf_op jit(solution)/shard_map/stack | solution.py:153
  30.9 3.0 collective-permute-start
  35.3 3.6 collective-permute-start.4
  40.6 7.1 collective-permute-start.7
  49.8 3.9 collective-permute-start.3
  56.7 4.8 collective-permute-done.3
  61.6 3.4 collective-permute-done.2
  66.6 8.3 add_add_fusion.1
  76.0 104.6 %all-gather.2.cloned.1.call-done = f32[2048,128]{1,0:T(8,128)} async-done(((f32[16,128]{1,0:T(8,128)}), f32[2048,128]{1,0:T(8,128)}) %all-gather.2.cloned.1.call-update) | async-done | bytes 1048592 | tf_op jit(solution)/shard_map/all_gather | solution.py:123
  184.3 171.3 %scatter_custom_fusion.1 = f32[32768]{0:T(1024)S(1)} fusion(s32[32768]{0:T(1024)} %bitcast.99, f32[32768]{0:T(1024)S(1)} %get-tuple-element.136, f32[]{:T(128)} %constant.189.clone.1), kind=kCustom, calls=%fused_computation.301 | custom fusion | flops 32768 | bytes 131584 | tf_op jit(solution)/shard_map/scatter-add | solution.py:131
  357.2 171.2 %scatter_custom_fusion = f32[32768]{0:T(1024)S(1)} fusion(s32[32768]{0:T(1024)} %bitcast.100, f32[32768]{0:T(1024)} %get-tuple-element.134, f32[]{:T(128)} %constant.189.clone.1), kind=kCustom, calls=%fused_computation.303 | custom fusion | flops 32768 | bytes 131584 | tf_op jit(solution)/shard_map/scatter-add | solution.py:136
  540.3 3.4 collective-permute-start.10
  550.8 3.0 collective-permute-start.12
  556.7 3.9 collective-permute-start.14
  567.5 3.1 collective-permute-start.20
  571.9 5.1 collective-permute-start.16
  579.9 3.9 collective-permute-start.18
  585.8 4.1 collective-permute-start.22
  605.2 3.9 collective-permute-start.26
  614.3 4.8 collective-permute-start.28
  621.9 3.9 collective-permute-start.30
  629.7 13.9 %all_gather.8 = f32[4,64,512]{2,1,0:T(8,128)S(1)} all-gather(f32[1,64,512]{2,1,0:T(8,128)S(1)} %slice_select_fusion), channel_id=1, replica_groups=mesh['tile'=128,'layer'=4] {'layer'}, dimensions={0}, use_global_device_ids=true | all-gather | bytes 655360 | tf_op jit(solution)/shard_map/all_gather | solution.py:37
  643.7 33.5 %while.15 = (s32[]{:T(128)}, f32[16,512]{1,0:T(8,128)S(1)}, s32[16,512]{1,0:T(8,128)S(1)}, f32[64,512]{1,0:T(8,128)S(1)}, s32[]{:T(128)}, /*index=5*/s32[]{:T(128)}) while((s32[]{:T(128)}, f32[16,512]{1,0:T(8,128)S(1)}, s32[16,512]{1,0:T(8,128)S(1)}, f32[64,512]{1,0:T(8,128)S(1)}, s32[]{:T(128)}, /*index=5*/s32[]{:T(128)}) %tuple.130), condition=%wide.region_5.6_spmd.clone, body=%wide.region_3.5_spmd.clone.sunk | while | flops 1074690 | bytes 3175509 | solution.py:93
  679.9 280.7 %reduce-scatter.2.cloned.1.call-done = f32[16,32]{1,0:T(8,128)} async-done(((f32[2048,32]{1,0:T(8,128)}), f32[16,32]{1,0:T(8,128)}) %reduce-scatter.2.cloned.1.call-update) | async-done | bytes 2064 | tf_op jit(solution)/shard_map/reduce_scatter | solution.py:175
  (290 shorter events, 118.4 us)
Async XLA Ops:
  7.2 173.4 %all-gather.2.cloned.1.call-start = ((), (), s32[]{:S(2)}) async-start(), calls=%async_computation.1 | async-start | bytes 1056768 | tf_op jit(solution)/shard_map/all_gather | solution.py:123
  29.6 20.0 %collective-permute-start.1 = (f32[2,2,1,512]{3,2,1,0:T(1,128)S(1)}, f32[2,2,1,512]{3,2,1,0:T(1,128)S(1)}, u32[]{:S(2)}, u32[]{:S(2)}) collective-permute-start(f32[2,2,1,512]{3,2,1,0:T(1,128)S(1)} %get-tuple-element.168), channel_id=1, source_target_pairs={{4,0},{8,4},{12,8},{16,12},{20,16},{24,20},{28,24},{32,28},{36,32}... | collective-permute-start | bytes 24584 | tf_op jit(solution)/shard_map/ppermute | solution.py:29
  30.9 18.7 %collective-permute-start = (f32[2,2,1,512]{3,2,1,0:T(1,128)S(1)}, f32[2,2,1,512]{3,2,1,0:T(1,128)S(1)}, u32[]{:S(2)}, u32[]{:S(2)}) collective-permute-start(f32[2,2,1,512]{3,2,1,0:T(1,128)S(1)} %get-tuple-element.167), channel_id=1, source_target_pairs={{0,4},{4,8},{8,12},{12,16},{16,20},{20,24},{24,28},{28,32},{32,36}... | collective-permute-start | bytes 24584 | tf_op jit(solution)/shard_map/ppermute | solution.py:26
  34.0 6.5 collective-permute-start.5
  39.0 921.7 %reduce-scatter.2.cloned.1.call-start = ((), (), s32[]{:S(2)}) async-start(), calls=%async_computation.2 | async-start | bytes 1056768 | tf_op jit(solution)/shard_map/reduce_scatter | solution.py:175
  40.6 15.8 %collective-permute-start.7 = (f32[1,66,512]{2,1,0:T(8,128)S(1)}, f32[1,66,512]{2,1,0:T(8,128)S(1)}, u32[]{:S(2)}, u32[]{:S(2)}) collective-permute-start(f32[1,66,512]{2,1,0:T(8,128)S(1)} %get-tuple-element.180), channel_id=1, source_target_pairs={{1,0},{2,1},{3,2},{5,4},{6,5},{7,6},{9,8},{10,9},{11,10},{13,12},{... | collective-permute-start | bytes 405512 | tf_op jit(solution)/shard_map/ppermute | solution.py:29
  47.7 8.7 collective-permute-start.6
  49.8 11.8 %collective-permute-start.3 = (f32[2,1,66,512]{3,2,1,0:T(8,128)S(1)}, f32[2,1,66,512]{3,2,1,0:T(8,128)S(1)}, u32[]{:S(2)}, u32[]{:S(2)}) collective-permute-start(f32[2,1,66,512]{3,2,1,0:T(8,128)S(1)} %get-tuple-element.164), channel_id=1, source_target_pairs={{1,0},{2,1},{3,2},{5,4},{6,5},{7,6},{9,8},{10,9},{11,10},{13,12},{... | collective-permute-start | bytes 811016 | tf_op jit(solution)/shard_map/ppermute | solution.py:29
  53.7 11.2 %collective-permute-start.2 = (f32[2,1,66,512]{3,2,1,0:T(8,128)S(1)}, f32[2,1,66,512]{3,2,1,0:T(8,128)S(1)}, u32[]{:S(2)}, u32[]{:S(2)}) collective-permute-start(f32[2,1,66,512]{3,2,1,0:T(8,128)S(1)} %get-tuple-element.163), channel_id=1, source_target_pairs={{0,1},{1,2},{2,3},{4,5},{5,6},{6,7},{8,9},{9,10},{10,11},{12,13},{... | collective-permute-start | bytes 811016 | tf_op jit(solution)/shard_map/ppermute | solution.py:26
  537.8 8.2 collective-permute-start.11
  540.3 8.4 collective-permute-start.10
  554.7 7.9 collective-permute-start.15
  556.7 7.9 collective-permute-start.14
  566.2 10.9 %collective-permute-start.21 = (f32[2,1,512]{2,1,0:T(1,128)S(1)}, f32[2,1,512]{2,1,0:T(1,128)S(1)}, u32[]{:S(2)}, u32[]{:S(2)}) collective-permute-start(f32[2,1,512]{2,1,0:T(1,128)S(1)} %get-tuple-element.186), channel_id=1, source_target_pairs={{4,0},{8,4},{12,8},{16,12},{20,16},{24,20},{28,24},{32,28},{36,32}... | collective-permute-start | bytes 12296 | tf_op jit(solution)/shard_map/ppermute | solution.py:29
  567.5 9.6 collective-permute-start.20
  570.6 6.5 collective-permute-start.17
  578.0 16.8 %collective-permute-start.19 = (f32[2,1,66,512]{3,2,1,0:T(8,128)S(1)}, f32[2,1,66,512]{3,2,1,0:T(8,128)S(1)}, u32[]{:S(2)}, u32[]{:S(2)}) collective-permute-start(f32[2,1,66,512]{3,2,1,0:T(8,128)S(1)} %get-tuple-element.162), channel_id=1, source_target_pairs={{1,0},{2,1},{3,2},{5,4},{6,5},{7,6},{9,8},{10,9},{11,10},{13,12},{... | collective-permute-start | bytes 811016 | tf_op jit(solution)/shard_map/ppermute | solution.py:29
  579.9 14.9 %collective-permute-start.18 = (f32[2,1,66,512]{3,2,1,0:T(8,128)S(1)}, f32[2,1,66,512]{3,2,1,0:T(8,128)S(1)}, u32[]{:S(2)}, u32[]{:S(2)}) collective-permute-start(f32[2,1,66,512]{3,2,1,0:T(8,128)S(1)} %get-tuple-element.161), channel_id=1, source_target_pairs={{0,1},{1,2},{2,3},{4,5},{5,6},{6,7},{8,9},{9,10},{10,11},{12,13},{... | collective-permute-start | bytes 811016 | tf_op jit(solution)/shard_map/ppermute | solution.py:26
  583.9 8.7 collective-permute-start.23
  585.8 8.7 collective-permute-start.22
  603.2 7.2 collective-permute-start.27
  605.2 7.0 collective-permute-start.26
  619.9 7.0 collective-permute-start.31
  621.9 7.0 collective-permute-start.30
  (34 other events, 457.0 us)
Sparse Core Ops, SparseCore 0:
  39.1 141.4 all-gather.1
  680.1 280.5 reduce-scatter.1
